TPU v7x, 32 devices: a whole 2x2x4 slice. The times are simulated.
32 devices in a mesh: dp: 2 (over y), seq: 4 (over z), chan: 4 (over x, core).
Axes of the slice: x: 2, y: 2, z: 4, core: 2. Of those that a mesh axis runs over, the one named last changes fastest.
Arguments:
- tokens: bfloat16 [16384, 1024], P(('dp', 'seq'), 'chan'), may hold values from -6 to 6
- gain_one: bfloat16 [1024], P('chan'), may hold values from 0.25 to 1.75
- in_weight: bfloat16 [1024, 3, 1024], P(None, None, 'chan'), may hold values from -0.1875 to 0.1875
- conv_weight: bfloat16 [3, 1024], P(None, 'chan'), may hold values from -3 to 3
- out_weight: bfloat16 [1024, 1024], P('chan'), may hold values from -0.1875 to 0.1875
- gain_two: bfloat16 [1024], replicated, may hold values from 0.25 to 1.75
- gate_up_weight: bfloat16 [1024, 2, 4608], P(None, None, 'chan'), may hold values from -0.1875 to 0.1875
- down_weight: bfloat16 [4608, 1024], P('chan'), may hold values from -0.09375 to 0.09375
- cotangent: bfloat16 [16384, 1024], P(('dp', 'seq'), 'chan'), may hold values from -6 to 6
Outputs:
- result: bfloat16 [16384, 1024], P(('dp', 'seq'), 'chan')
- grad_tokens: bfloat16 [16384, 1024], P(('dp', 'seq'), 'chan')
- grad_gain_one: float32 [1024], P('chan')
- grad_in_weight: float32 [1024, 3, 1024], P(None, None, 'chan')
- grad_conv_weight: float32 [3, 1024], P(None, 'chan')
- grad_out_weight: float32 [1024, 1024], P('chan')
- grad_gain_two: float32 [1024], P('chan')
- grad_gate_up: float32 [1024, 2, 4608], P(None, None, 'chan')
- grad_down: float32 [4608, 1024], P('chan')
All inputs are finite; a program needn't handle non-finite values.
Results may differ from a plain program's by a relative error of at most 0.018.
Values may be sent and summed in bfloat16 or wider, within the bound.
No kernel may reach another device: no remote copies, remote signals or barrier semaphores. Data moves between devices by JAX's collectives and lax.ppermute only.
A program may use at most 256 MiB of HBM per device.

v0:
```python
import jax
import jax.numpy as jnp
from jax import lax
from jax.sharding import PartitionSpec as P

epsilon = 1e-05


def shifted(value, axis, by):
    length = lax.axis_size(axis)
    pairs = [(i, i + by) for i in range(length) if 0 <= i + by < length]
    return lax.ppermute(value, axis, pairs)


def shards(
    tokens,
    gain_one,
    in_weight,
    conv_weight,
    out_weight,
    gain_two,
    gate_up_weight,
    down_weight,
    cotangent,
):
    width = in_weight.shape[0]
    local_width = in_weight.shape[2]
    hidden_local = gate_up_weight.shape[2]
    count = tokens.shape[0]
    offset = lax.axis_index("chan") * local_width
    in_flat = in_weight.reshape(width, 3 * local_width)
    gu_flat = gate_up_weight.reshape(width, 2 * hidden_local)
    kernel = conv_weight.astype(jnp.float32)
    gain_second = gain_two.astype(jnp.float32)
    tokens_local = tokens.astype(jnp.float32)
    tokens_full, gain_full = (
        lax.all_gather(tokens, "chan", axis=1, tiled=True),
        lax.all_gather(gain_one, "chan", axis=0, tiled=True),
    )
    x_float = tokens_full.astype(jnp.float32)
    inv_one = lax.rsqrt(jnp.mean(x_float * x_float, axis=-1, keepdims=True) + epsilon)
    normed_one = (x_float * inv_one * gain_full.astype(jnp.float32)).astype(jnp.bfloat16)
    projected = jnp.dot(normed_one, in_flat, preferred_element_type=jnp.float32)
    gate_b = projected[:, :local_width]
    gate_c = projected[:, local_width : 2 * local_width]
    values = projected[:, 2 * local_width :]
    product = gate_b * values
    state = shifted(product[count - 2 :], "seq", 1)
    extended = jnp.concatenate([state, product], axis=0)
    conv_out = (
        kernel[0] * extended[0:count]
        + kernel[1] * extended[1 : count + 1]
        + kernel[2] * extended[2 : count + 2]
    )
    mixed = (gate_c * conv_out).astype(jnp.bfloat16)
    mix_partial = jnp.dot(mixed, out_weight, preferred_element_type=jnp.float32)
    resid = x_float + lax.psum(mix_partial, "chan")
    inv_two = lax.rsqrt(jnp.mean(resid * resid, axis=-1, keepdims=True) + epsilon)
    scaled_two = resid * inv_two
    normed_two = (scaled_two * gain_second).astype(jnp.bfloat16)
    resid_local = lax.dynamic_slice_in_dim(resid, offset, local_width, 1)
    gate_up = jnp.dot(normed_two, gu_flat, preferred_element_type=jnp.float32)
    gate_pre = gate_up[:, :hidden_local]
    up_pre = gate_up[:, hidden_local:]
    sigma = jax.nn.sigmoid(gate_pre)
    hidden = (gate_pre * sigma * up_pre).astype(jnp.bfloat16)
    ffn_local = lax.psum_scatter(
        jnp.dot(hidden, down_weight, preferred_element_type=jnp.float32).astype(jnp.bfloat16),
        "chan",
        scatter_dimension=1,
        tiled=True,
    ).astype(jnp.float32)
    result = (resid_local + ffn_local).astype(jnp.bfloat16)
    cot_full = lax.all_gather(cotangent, "chan", axis=1, tiled=True)
    d_hidden = jnp.dot(cot_full, down_weight.T, preferred_element_type=jnp.float32)
    grad_down = jnp.dot(hidden.T, cot_full, preferred_element_type=jnp.float32)
    d_gate = d_hidden * up_pre * sigma * (1.0 + gate_pre * (1.0 - sigma))
    d_up = d_hidden * gate_pre * sigma
    d_gate_up = jnp.concatenate([d_gate, d_up], axis=1).astype(jnp.bfloat16)
    grad_gate_up = jnp.dot(normed_two.T, d_gate_up, preferred_element_type=jnp.float32).reshape(
        width, 2, hidden_local
    )
    norm_partial = jnp.dot(d_gate_up, gu_flat.T, preferred_element_type=jnp.float32)
    d_norm_two = lax.psum(norm_partial, "chan")
    grad_gain_two = lax.dynamic_slice_in_dim(
        jnp.sum(d_norm_two * scaled_two, axis=0), offset, local_width, 0
    )
    pulled_two = d_norm_two * gain_second
    d_resid = cot_full.astype(jnp.float32) + inv_two * (
        pulled_two - scaled_two * jnp.mean(pulled_two * scaled_two, axis=-1, keepdims=True)
    )
    d_out = d_resid.astype(jnp.bfloat16)
    d_resid_local = lax.dynamic_slice_in_dim(d_resid, offset, local_width, 1)
    d_mixed = jnp.dot(d_out, out_weight.T, preferred_element_type=jnp.float32)
    grad_out = jnp.dot(mixed.T, d_out, preferred_element_type=jnp.float32)
    d_gate_c = d_mixed * conv_out
    d_conv = d_mixed * gate_c
    next_grad = shifted(d_conv[0:2], "seq", -1)
    grad_ext = jnp.concatenate([d_conv, next_grad], axis=0)
    d_product = (
        kernel[2] * grad_ext[0:count]
        + kernel[1] * grad_ext[1 : count + 1]
        + kernel[0] * grad_ext[2 : count + 2]
    )
    grad_conv = jnp.stack(
        [
            jnp.sum(d_conv * extended[shift_index : shift_index + count], axis=0)
            for shift_index in range(3)
        ]
    )
    d_project = jnp.concatenate([d_product * values, d_gate_c, d_product * gate_b], axis=1).astype(
        jnp.bfloat16
    )
    grad_in = jnp.dot(normed_one.T, d_project, preferred_element_type=jnp.float32).reshape(
        width, 3, local_width
    )
    d_norm_one = lax.psum_scatter(
        jnp.dot(d_project, in_flat.T, preferred_element_type=jnp.float32).astype(jnp.bfloat16),
        "chan",
        scatter_dimension=1,
        tiled=True,
    ).astype(jnp.float32)
    scaled_one = tokens_local * inv_one
    grad_gain_one = jnp.sum(d_norm_one * scaled_one, axis=0)
    pulled_one = d_norm_one * gain_one.astype(jnp.float32)
    inner_sum = lax.psum(jnp.sum(pulled_one * scaled_one, axis=-1, keepdims=True), "chan")
    grad_tokens = (
        d_resid_local + inv_one * (pulled_one - scaled_one * (inner_sum / width))
    ).astype(jnp.bfloat16)
    grad_gain_one, grad_in, grad_conv, grad_out, grad_gain_two, grad_gate_up, grad_down = (
        lax.psum(grad_gain_one.astype(jnp.bfloat16), ("dp", "seq")).astype(jnp.float32),
        lax.psum(grad_in.astype(jnp.bfloat16), ("dp", "seq")).astype(jnp.float32),
        lax.psum(grad_conv.astype(jnp.bfloat16), ("dp", "seq")).astype(jnp.float32),
        lax.psum(grad_out.astype(jnp.bfloat16), ("dp", "seq")).astype(jnp.float32),
        lax.psum(grad_gain_two.astype(jnp.bfloat16), ("dp", "seq")).astype(jnp.float32),
        lax.psum(grad_gate_up.astype(jnp.bfloat16), ("dp", "seq")).astype(jnp.float32),
        lax.psum(grad_down.astype(jnp.bfloat16), ("dp", "seq")).astype(jnp.float32),
    )
    return (
        result,
        grad_tokens,
        grad_gain_one,
        grad_in,
        grad_conv,
        grad_out,
        grad_gain_two,
        grad_gate_up,
        grad_down,
    )


def solution(mesh):
    placed = (
        P(("dp", "seq"), "chan"),
        P("chan"),
        P(None, None, "chan"),
        P(None, "chan"),
        P("chan", None),
        P(),
        P(None, None, "chan"),
        P("chan", None),
        P(("dp", "seq"), "chan"),
    )
    return jax.shard_map(
        shards,
        mesh=mesh,
        in_specs=placed,
        out_specs=(
            P(("dp", "seq"), "chan"),
            P(("dp", "seq"), "chan"),
            P("chan"),
            P(None, None, "chan"),
            P(None, "chan"),
            P("chan", None),
            P("chan"),
            P(None, None, "chan"),
            P("chan", None),
        ),
        check_vma=False,
    )
```

profile of v0, /device:TPU:0, one launch (start us, length us, event | category | flops | bytes accessed | tf_op | source)
XLA Modules:
  0.0 858.1 jit_solution(401732263966881372)
XLA Ops:
  8.0 2.6 copy.25
  10.6 6.0 all-gather
  16.6 30.7 %all-gather.4.cloned.1.call-done = bf16[2048,1024]{1,0:T(8,128)(2,1)} async-done(((bf16[2048,256]{1,0:T(8,128)(2,1)}), bf16[2048,1024]{1,0:T(8,128)(2,1)}) %all-gather.4.cloned.1.call-update) | async-done | bytes 4194320 | tf_op jit(solution)/shard_map/all_gather | solution.py:37
  47.3 3.2 fusion
  50.8 5.0 fusion.27
  56.1 3.5 collective-permute-start
  59.7 1.3 collective-permute-done
  61.0 2.0 multiply_convert_fusion.7
  63.0 1.0 copy-done.10
  64.0 4.7 fusion.36
  69.8 5.4 copy.30
  75.1 147.3 %all-reduce.6.cloned.1.call-done = f32[2048,1024]{1,0:T(8,128)} async-done(((f32[2048,1024]{1,0:T(8,128)}), f32[2048,1024]{1,0:T(8,128)}) %all-reduce.6.cloned.1.call-update) | async-done | bytes 8388624 | tf_op jit(solution)/shard_map/psum | solution.py:57
  222.5 5.7 multiply_reduce_fusion.2
  228.2 3.4 copy-done.3
  231.6 16.3 %fusion.33 = f32[2048,2304]{1,0:T(8,128)} fusion(bf16[1024,2304]{1,0:T(8,128)(2,1)} %bitcast.27, f32[2048,1024]{1,0:T(8,128)S(1)} %get-tuple-element.27, f32[1024]{0:T(1024)S(1)} %convert_element_type.107, f32[2048]{0:T(1024)S(1)} %add_rsqrt_fusion), kind=kOutput, calls=%fused_computation.73 | convolution fusion | flops 9669967872 | bytes 31993856 | tf_op jit(solution)/shard_map/dot_general | solution.py:62
  247.9 11.3 %all-gather.6.cloned.1.call-done = bf16[2048,1024]{1,0:T(8,128)(2,1)} async-done(((bf16[2048,256]{1,0:T(8,128)(2,1)}), bf16[2048,1024]{1,0:T(8,128)(2,1)}) %all-gather.6.cloned.1.call-update) | async-done | bytes 4194320 | tf_op jit(solution)/shard_map/all_gather | solution.py:74
  259.2 18.2 %multiply_convert_fusion.1 = (bf16[2048,1152]{1,0:T(8,128)(2,1)}, bf16[2048,1152]{1,0:T(8,128)(2,1)}, bf16[2048,1152]{1,0:T(8,128)(2,1)}) fusion(f32[2048,2304]{1,0:T(8,128)} %fusion.33, bf16[2048,1024]{1,0:T(8,128)(2,1)} %all-gather.6.cloned.1.call-done, bf16[1152,1024]{1,0:T(8,128)(2,1)S(1)} %copy-done), kind=kOutput, calls=%fused_computation.5 | convolution fusion | flops 4869586944 | bytes 39583744 | tf_op jit(solution)/shard_map/dot_general | solution.py:75
  277.4 15.8 %fusion.4 = f32[2048,1024]{1,0:T(8,128)} fusion(bf16[1024,2304]{1,0:T(8,128)(2,1)} %bitcast.28, bf16[2048,1152]{1,0:T(8,128)(2,1)} %get-tuple-element.31, bf16[2048,1152]{1,0:T(8,128)(2,1)} %get-tuple-element.30), kind=kOutput, calls=%fused_computation.17 | convolution fusion | flops 9682550784 | bytes 22544384 | tf_op jit(solution)/shard_map/dot_general | solution.py:83
  293.9 9.5 %convolution_convert_fusion.1 = bf16[2048,1024]{1,0:T(8,128)(2,1)} fusion(bf16[2048,1152]{1,0:T(8,128)(2,1)} %get-tuple-element.32, bf16[1152,1024]{1,0:T(8,128)(2,1)S(1)} %copy-done), kind=kOutput, calls=%fused_computation.20 | convolution fusion | flops 4833935360 | bytes 11272192 | tf_op jit(solution)/shard_map/dot_general | solution.py:68
  303.5 142.9 %all-reduce.8.cloned.1.call-done = f32[2048,1024]{1,0:T(8,128)} async-done(((f32[2048,1024]{1,0:T(8,128)}), f32[2048,1024]{1,0:T(8,128)}) %all-reduce.8.cloned.1.call-update) | async-done | bytes 8388624 | tf_op jit(solution)/shard_map/psum | solution.py:84
  446.3 7.1 multiply_reduce_fusion
  453.4 1.4 copy-done.4
  454.9 7.7 multiply_add_fusion
  462.6 2.9 fusion.21
  465.5 1.4 copy-done.2
  466.9 1.4 copy-done.13
  468.2 1.1 multiply_reduce_fusion.5
  469.4 1.3 collective-permute-start.1
  470.7 4.2 collective-permute-done.1
  477.0 0.9 copy-done.16
  477.8 5.0 convolution_convert_fusion.2
  483.0 16.9 %fusion.5 = bf16[1024,2304]{1,0:T(8,128)(2,1)} fusion(bf16[2048,1152]{1,0:T(8,128)(2,1)} %get-tuple-element.31, bf16[2048,1152]{1,0:T(8,128)(2,1)} %get-tuple-element.30, f32[2048,1024]{1,0:T(8,128)} %copy-done.3, f32[1024]{0:T(1024)S(1)} %convert_element_type.107, f32[2048]{0:T(1024)S(1)} %add_rsqrt_fusion), kind=kOutput, calls=%fused_computation.18 | convolution fusion | flops 9691201536 | bytes 22556672 | tf_op jit(solution)/shard_map/dot_general | solution.py:80
  500.0 10.3 %convert_element_type.131 = bf16[1024,2,1152]{2,1,0:T(2,128)(2,1)} reshape(bf16[1024,2304]{1,0:T(8,128)(2,1)} %fusion.5) | data formatting | bytes 9437184 | tf_op jit(solution)/shard_map/convert_element_type | solution.py:136
  510.3 9.6 %convolution_convert_fusion = bf16[1152,1024]{1,0:T(8,128)(2,1)} fusion(bf16[2048,1152]{1,0:T(8,128)(2,1)} %get-tuple-element.32, bf16[2048,1024]{1,0:T(8,128)(2,1)} %all-gather.6.cloned.1.call-done), kind=kOutput, calls=%fused_computation.19 | convolution fusion | flops 4833017856 | bytes 11272192 | tf_op jit(solution)/shard_map/dot_general | solution.py:76
  519.9 5.6 fusion.23
  525.6 4.0 convolution_convert_fusion.3
  529.6 1.6 copy.28
  531.9 3.2 add_convert_fusion
  535.1 5.0 reduce-scatter.5.cloned.1.call-done
  540.1 2.1 fusion.17
  542.2 22.3 %all-reduce = (bf16[256]{0:T(256)(128)(2,1)S(1)}, bf16[3,256]{1,0:T(4,128)(2,1)S(1)}, bf16[256]{0:T(256)(128)(2,1)S(1)}) all-reduce(bf16[256]{0:T(256)(128)(2,1)S(1)} %get-tuple-element.14, bf16[3,256]{1,0:T(4,128)(2,1)S(1)} %pad_maximum_fusion.10, ...), channel_id=1, replica_groups=mesh['dp'=2,'seq'=4,'chan'=4] {'dp','seq'}, use_global_device_ids=true, to_apply=%region_10.0 | all-reduce | flops 1280 | bytes 5120 | tf_op jit(solution)/shard_map/psum | solution.py:131
  566.3 6.1 psum.72
  572.4 3.1 fusion.16
  575.6 262.1 %all-reduce.10.cloned.1.call-done = (bf16[1024,3,256]{2,0,1:T(8,128)(2,1)}, bf16[256,1024]{1,0:T(8,128)(2,1)}, bf16[1024,2,1152]{2,1,0:T(2,128)(2,1)}, bf16[1152,1024]{1,0:T(8,128)(2,1)}) async-done(((bf16[1024,3,256]{2,0,1:T(8,128)(2,1)}, bf16[256,1024]{1,0:T(8,128)(2,1)}, bf16[1024,2,1152]{2,1,0:T(2,128)(2,1)}, bf16[1152,1024]{1,0:T(8,128)(2,1)}), (bf16[1024,3,256]{2,0,1:T(8,128)(2,1)}, ...) | async-done | bytes 9175056 | tf_op jit(solution)/shard_map/psum | solution.py:132
  837.7 7.3 convert_element_type.132
  845.0 2.9 convert_element_type.134
  848.0 1.9 convert_element_type.124
  849.9 1.1 convert_element_type.127
  (98 shorter events, 8.0 us)
Async XLA Ops:
  7.2 252.0 %copy-start = (bf16[1152,1024]{1,0:T(8,128)(2,1)S(1)}, bf16[1152,1024]{1,0:T(8,128)(2,1)}, u32[]{:S(2)}) copy-start(bf16[1152,1024]{1,0:T(8,128)(2,1)} %param.16) | copy-start | bytes 7077892
  7.2 3.4 copy-start.29
  7.2 40.1 %all-gather.4.cloned.1.call-start = ((), (), s32[]{:S(2)}) async-start(), calls=%async_computation.2 | async-start | bytes 5242880 | tf_op jit(solution)/shard_map/all_gather | solution.py:37
  7.9 214.5 %all-reduce.6.cloned.1.call-start = ((), (), s32[]{:S(2)}) async-start(), calls=%async_computation.3 | async-start | bytes 16777216 | tf_op jit(solution)/shard_map/psum | solution.py:57
  16.6 39.2 %copy-start.26 = (f32[4,1,256]{2,1,0:T(1,128)}, f32[4,1,256]{2,1,0:T(1,128)S(1)}, u32[]{:S(2)}) copy-start(f32[4,1,256]{2,1,0:T(1,128)S(1)} %convert_element_type.135) | copy-start | bytes 12292
  47.3 3.4 copy-start.8
  50.6 5.2 copy-start.23
  55.8 7.2 copy-start.5
  55.8 3.9 copy-start.25
  56.1 6.9 copy-start.6
  56.1 7.9 copy-start.15
  56.1 4.8 collective-permute-start
  63.0 1.0 copy-start.10
  68.6 1.1 copy-start.28
  68.7 190.5 %all-gather.6.cloned.1.call-start = ((), (), s32[]{:S(2)}) async-start(), calls=%async_computation.5 | async-start | bytes 5242880 | tf_op jit(solution)/shard_map/all_gather | solution.py:74
  69.4 376.9 %all-reduce.8.cloned.1.call-start = ((), (), s32[]{:S(2)}) async-start(), calls=%async_computation.6 | async-start | bytes 16777216 | tf_op jit(solution)/shard_map/psum | solution.py:84
  228.2 3.4 copy-start.3
  293.3 238.6 %reduce-scatter.3.cloned.1.call-start = ((), (), s32[]{:S(2)}) async-start(), calls=%async_computation.4 | async-start | bytes 5242880 | tf_op jit(solution)/shard_map/reduce_scatter | solution.py:67
  303.4 236.7 %reduce-scatter.5.cloned.1.call-start = ((), (), s32[]{:S(2)}) async-start(), calls=%async_computation.7 | async-start | bytes 5242880 | tf_op jit(solution)/shard_map/reduce_scatter | solution.py:117
  446.3 8.5 copy-start.4
  446.3 20.5 %slice-start = ((s8[6291456]{0:T(1024)(128)(4,1)}), s8[4194304]{0:T(1024)(128)(4,1)S(1)}, s32[]{:S(2)}) async-start(s8[6291456]{0:T(1024)(128)(4,1)} %bitcast.24), calls=%async_computation.9 | async-start | bytes 8388608
  454.9 12.0 %slice-start.1 = ((s8[6291456]{0:T(1024)(128)(4,1)}), s8[2097152]{0:T(1024)(128)(4,1)S(1)}, s32[]{:S(2)}) async-start(s8[6291456]{0:T(1024)(128)(4,1)} %bitcast.24), calls=%async_computation.10 | async-start | bytes 4194304
  462.6 4.3 copy-start.2
  462.6 4.3 copy-start.7
  462.6 5.6 copy-start.13
  469.4 5.5 collective-permute-start.1
  475.6 1.0 copy-start.18
  475.6 2.2 copy-start.16
  476.0 1.0 copy-start.20
  482.8 354.9 %all-reduce.10.cloned.1.call-start = ((), (), s32[]{:S(2)}) async-start(), calls=%async_computation.8 | async-start | bytes 18350080 | tf_op jit(solution)/shard_map/psum | solution.py:132
  510.3 9.6 %copy-start.11 = (bf16[2048,256]{1,0:T(8,128)(2,1)S(1)}, bf16[2048,256]{1,0:T(8,128)(2,1)}, u32[]{:S(2)}) copy-start(bf16[2048,256]{1,0:T(8,128)(2,1)} %copy-done.10) | copy-start | bytes 3145732
  519.8 5.7 copy-start.9
  519.9 5.7 copy-start.19
  519.9 5.7 copy-start.21
  519.9 5.7 copy-start.24
  519.9 5.7 copy-start.27
  531.1 0.7 copy-start.30
  531.8 8.3 copy-start.12
  837.7 7.3 copy-start.14
  845.0 3.0 copy-start.17
  845.0 4.9 copy-start.22
  845.0 6.0 copy-start.1
Sparse Core Ops, SparseCore 0:
  9.6 37.7 all-gather.3
  68.8 153.6 all-reduce.5
  224.0 35.1 all-gather.5
  293.4 152.8 all-reduce.7
  448.7 44.5 reduce-scatter.2
  495.7 44.3 reduce-scatter.4
  545.9 291.7 all-reduce.9
where the time goes:
time: 864 us; the launch traced here: 858 us
  waiting for transfers between devices  606 us (70%)
  matrix products  114 us (13%)
  other arithmetic  51.8 us (6%)
  blocking collectives  34.5 us (4%)
  local copies, waits for them, and re-layouts  31.2 us (4%)
  between operations  14.8 us (2%)
    psum x1, waiting for transfers between devices, shards(): lax.psum(grad_in.astype(jnp.bfloat16), ('dp', 'seq')).astype(jnp.float32)  262 us
    psum x1, waiting for transfers between devices, shards(): resid = x_float + lax.psum(mix_partial, 'chan')  147 us
    psum x1, waiting for transfers between devices, shards(): d_norm_two = lax.psum(norm_partial, 'chan')  143 us
    all_gather x1, waiting for transfers between devices, shards(): lax.all_gather(tokens, 'chan', axis=1, tiled=True)  30.7 us
    psum x1, blocking collectives, shards(): lax.psum(grad_gain_one.astype(jnp.bfloat16), ('dp', 'seq'))  22.3 us
    unnamed x69, local copies, waits for them, and re-layouts  19.2 us
    dot_general x1, matrix products, shards(): jnp.dot(cot_full, down_weight.T, preferred_element_type=jnp.float32)  18.2 us
  transfers between devices with their start and end apart: 9, of which 8 were waited for; matrix products, arithmetic and copies ran while one was open for 14% of the time, Pallas kernels for 0%

commit v1 on v0

--- a/solution.py
+++ b/solution.py
@@ -4,6 +4,14 @@
 from jax.sharding import PartitionSpec as P
 
 epsilon = 1e-05
+
+
+def time_pools(obj):
+    along_axis = "seq"
+    row_axis = "dp"
+    for to_i in (row_axis, along_axis):
+        obj = lax.psum(obj, to_i)
+    return obj
 
 
 def shifted(value, axis, by):
@@ -129,7 +137,7 @@
     ).astype(jnp.bfloat16)
     grad_gain_one, grad_in, grad_conv, grad_out, grad_gain_two, grad_gate_up, grad_down = (
         lax.psum(grad_gain_one.astype(jnp.bfloat16), ("dp", "seq")).astype(jnp.float32),
-        lax.psum(grad_in.astype(jnp.bfloat16), ("dp", "seq")).astype(jnp.float32),
+        time_pools(grad_in.astype(jnp.bfloat16)).astype(jnp.float32),
         lax.psum(grad_conv.astype(jnp.bfloat16), ("dp", "seq")).astype(jnp.float32),
         lax.psum(grad_out.astype(jnp.bfloat16), ("dp", "seq")).astype(jnp.float32),
         lax.psum(grad_gain_two.astype(jnp.bfloat16), ("dp", "seq")).astype(jnp.float32),

time: 864 us -> 1000 us (1.16)
  waiting for transfers between devices: 606 us -> 739 us
    psum x1 -> x3, waiting for transfers between devices: 262 us -> 312 us  [the longest x1 251 us: shards(): lax.psum(grad_out.astype(jnp.bfloat16), ('dp', 'seq')).astype(jnp.float32)]
    reduce_scatter x1, waiting for transfers between devices: 0.02 us -> 42.8 us  [shards(): lax.psum_scatter(jnp.dot(hidden, down_weight, preferred_element_type=jnp....]
    reduce_scatter x1, waiting for transfers between devices: 4.97 us -> 34.8 us  [shards(): lax.psum_scatter(jnp.dot(d_project, in_flat.T, preferred_element_type=jnp...]
  transfers between devices with their start and end apart: 9 -> 11, of which waited for: 8 -> 11; matrix products, arithmetic and copies ran while one was open for 14% -> 11% of each run, Pallas kernels for 0% -> 0%
where the time goes in v1:
time: 1000 us; the launch traced here: 993 us
  waiting for transfers between devices  739 us (74%)
  matrix products  117 us (12%)
  other arithmetic  51.1 us (5%)
  blocking collectives  33.6 us (3%)
  local copies, waits for them, and re-layouts  32.3 us (3%)
  between operations  14.4 us (1%)
    psum x1, waiting for transfers between devices, shards(): lax.psum(grad_out.astype(jnp.bfloat16), ('dp', 'seq')).astype(jnp.float32)  251 us
    psum x1, waiting for transfers between devices, shards(): d_norm_two = lax.psum(norm_partial, 'chan')  153 us
    psum x1, waiting for transfers between devices, shards(): resid = x_float + lax.psum(mix_partial, 'chan')  147 us
    psum x2, waiting for transfers between devices, time_pools(): obj = lax.psum(obj, to_i)  61.7 us
    reduce_scatter x1, waiting for transfers between devices, shards(): lax.psum_scatter(jnp.dot(hidden, down_weight, preferred_element_type=jnp....  42.8 us
    reduce_scatter x1, waiting for transfers between devices, shards(): lax.psum_scatter(jnp.dot(d_project, in_flat.T, preferred_element_type=jnp...  34.8 us
    all_gather x1, waiting for transfers between devices, shards(): lax.all_gather(tokens, 'chan', axis=1, tiled=True)  30.7 us
    psum x1, blocking collectives, shards(): lax.psum(grad_gain_one.astype(jnp.bfloat16), ('dp', 'seq'))  21.5 us
  transfers between devices with their start and end apart: 11, of which 11 were waited for; matrix products, arithmetic and copies ran while one was open for 11% of the time, Pallas kernels for 0%

profile of v1, /device:TPU:0, one launch (start us, length us, event | category | flops | bytes accessed | tf_op | source)
XLA Modules:
  0.0 993.3 jit_solution(1072018315920068617)
XLA Ops:
  8.0 2.6 copy.25
  10.6 6.0 all-gather
  16.6 30.7 %all-gather.4.cloned.1.call-done = bf16[2048,1024]{1,0:T(8,128)(2,1)} async-done(((bf16[2048,256]{1,0:T(8,128)(2,1)}), bf16[2048,1024]{1,0:T(8,128)(2,1)}) %all-gather.4.cloned.1.call-update) | async-done | bytes 4194320 | tf_op jit(solution)/shard_map/all_gather | solution.py:45
  47.3 3.2 fusion
  50.8 5.0 fusion.27
  56.1 3.5 collective-permute-start
  59.7 1.3 collective-permute-done
  61.0 2.0 multiply_convert_fusion.7
  64.0 4.7 fusion.36
  70.0 5.5 copy.30
  75.5 147.0 %all-reduce.8.cloned.1.call-done = f32[2048,1024]{1,0:T(8,128)} async-done(((f32[2048,1024]{1,0:T(8,128)}), f32[2048,1024]{1,0:T(8,128)}) %all-reduce.8.cloned.1.call-update) | async-done | bytes 8388624 | tf_op jit(solution)/shard_map/psum | solution.py:65
  222.5 5.7 multiply_reduce_fusion.2
  228.2 3.4 copy-done.2
  231.6 16.3 %fusion.33 = f32[2048,2304]{1,0:T(8,128)} fusion(bf16[1024,2304]{1,0:T(8,128)(2,1)} %bitcast.27, f32[2048,1024]{1,0:T(8,128)S(1)} %get-tuple-element.26, f32[1024]{0:T(1024)S(1)} %convert_element_type.107, f32[2048]{0:T(1024)S(1)} %add_rsqrt_fusion), kind=kOutput, calls=%fused_computation.73 | convolution fusion | flops 9669967872 | bytes 31993856 | tf_op jit(solution)/shard_map/dot_general | solution.py:70
  247.9 11.3 %all-gather.6.cloned.1.call-done = bf16[2048,1024]{1,0:T(8,128)(2,1)} async-done(((bf16[2048,256]{1,0:T(8,128)(2,1)}), bf16[2048,1024]{1,0:T(8,128)(2,1)}) %all-gather.6.cloned.1.call-update) | async-done | bytes 4194320 | tf_op jit(solution)/shard_map/all_gather | solution.py:82
  259.2 18.2 %multiply_convert_fusion.1 = (bf16[2048,1152]{1,0:T(8,128)(2,1)}, bf16[2048,1152]{1,0:T(8,128)(2,1)}, bf16[2048,1152]{1,0:T(8,128)(2,1)}) fusion(f32[2048,2304]{1,0:T(8,128)} %fusion.33, bf16[2048,1024]{1,0:T(8,128)(2,1)} %all-gather.6.cloned.1.call-done, bf16[1152,1024]{1,0:T(8,128)(2,1)S(1)} %copy-done), kind=kOutput, calls=%fused_computation.5 | convolution fusion | flops 4869586944 | bytes 39583744 | tf_op jit(solution)/shard_map/dot_general | solution.py:83
  277.4 15.8 %fusion.4 = f32[2048,1024]{1,0:T(8,128)} fusion(bf16[1024,2304]{1,0:T(8,128)(2,1)} %bitcast.28, bf16[2048,1152]{1,0:T(8,128)(2,1)} %get-tuple-element.30, bf16[2048,1152]{1,0:T(8,128)(2,1)} %get-tuple-element.29), kind=kOutput, calls=%fused_computation.17 | convolution fusion | flops 9682550784 | bytes 22544384 | tf_op jit(solution)/shard_map/dot_general | solution.py:91
  293.5 152.8 %all-reduce.10.cloned.1.call-done = f32[2048,1024]{1,0:T(8,128)} async-done(((f32[2048,1024]{1,0:T(8,128)}), f32[2048,1024]{1,0:T(8,128)}) %all-reduce.10.cloned.1.call-update) | async-done | bytes 8388624 | tf_op jit(solution)/shard_map/psum | solution.py:92
  446.3 7.1 multiply_reduce_fusion
  453.4 1.1 copy-done.3
  454.5 5.9 multiply_add_fusion
  460.4 2.9 fusion.21
  463.3 1.3 copy-done.1
  464.7 1.2 copy-done.12
  466.9 1.3 collective-permute-start.1
  468.2 4.2 collective-permute-done.1
  473.5 2.6 copy-done.8
  476.1 5.1 convolution_convert_fusion.3
  481.2 2.6 copy.28
  483.8 50.9 %all-reduce.12.cloned.1.call-done = bf16[1024,3,256]{2,0,1:T(8,128)(2,1)} async-done(((bf16[1024,3,256]{2,0,1:T(8,128)(2,1)}), bf16[1024,3,256]{2,0,1:T(8,128)(2,1)}) %all-reduce.12.cloned.1.call-update) | async-done | bytes 1572880 | tf_op jit(solution)/shard_map/psum | solution.py:13
  534.8 9.6 convolution_convert_fusion.1
  544.6 16.9 %fusion.5 = bf16[1024,2304]{1,0:T(8,128)(2,1)} fusion(bf16[2048,1152]{1,0:T(8,128)(2,1)} %get-tuple-element.30, bf16[2048,1152]{1,0:T(8,128)(2,1)} %get-tuple-element.29, f32[2048,1024]{1,0:T(8,128)} %copy-done.2, f32[1024]{0:T(1024)S(1)} %convert_element_type.107, f32[2048]{0:T(1024)S(1)} %add_rsqrt_fusion), kind=kOutput, calls=%fused_computation.18 | convolution fusion | flops 9691201536 | bytes 22556672 | tf_op jit(solution)/shard_map/dot_general | solution.py:88
  561.6 10.1 %convert_element_type.131 = bf16[1024,2,1152]{2,1,0:T(2,128)(2,1)} reshape(bf16[1024,2304]{1,0:T(8,128)(2,1)} %fusion.5) | data formatting | bytes 9437184 | tf_op jit(solution)/shard_map/convert_element_type | solution.py:144
  571.6 9.4 convolution_convert_fusion
  581.0 5.5 fusion.23
  586.8 7.5 convolution_convert_fusion.2
  595.1 10.9 %all-reduce.14.cloned.1.call-done = bf16[1024,3,256]{2,0,1:T(8,128)(2,1)} async-done(((bf16[1024,3,256]{2,0,1:T(8,128)(2,1)}), bf16[1024,3,256]{2,0,1:T(8,128)(2,1)}) %all-reduce.14.cloned.1.call-update) | async-done | bytes 1572880 | tf_op jit(solution)/shard_map/psum | solution.py:13
  605.9 3.3 convert_element_type.124
  609.3 42.8 %reduce-scatter.3.cloned.1.call-done = bf16[2048,256]{1,0:T(8,128)(2,1)} async-done(((bf16[2048,1024]{1,0:T(8,128)(2,1)}), bf16[2048,256]{1,0:T(8,128)(2,1)}) %reduce-scatter.3.cloned.1.call-update) | async-done | bytes 1048592 | tf_op jit(solution)/shard_map/reduce_scatter | solution.py:75
  652.1 3.1 add_convert_fusion
  655.2 250.6 %all-reduce.16.cloned.1.call-done = (bf16[256,1024]{1,0:T(8,128)(2,1)}, bf16[1024,2,1152]{2,1,0:T(2,128)(2,1)}, bf16[1152,1024]{1,0:T(8,128)(2,1)}) async-done(((bf16[256,1024]{1,0:T(8,128)(2,1)}, bf16[1024,2,1152]{2,1,0:T(2,128)(2,1)}, bf16[1152,1024]{1,0:T(8,128)(2,1)}), (bf16[256,1024]{1,0:T(8,128)(2,1)}, bf16[1024,2,1152]{2,1,0:T(2,128)(2,1)}, ...) | async-done | bytes 7602192 | tf_op jit(solution)/shard_map/psum | solution.py:142
  905.8 7.3 convert_element_type.132
  913.1 2.9 convert_element_type.134
  917.2 34.8 %reduce-scatter.5.cloned.1.call-done = bf16[2048,256]{1,0:T(8,128)(2,1)} async-done(((bf16[2048,1024]{1,0:T(8,128)(2,1)}), bf16[2048,256]{1,0:T(8,128)(2,1)}) %reduce-scatter.5.cloned.1.call-update) | async-done | bytes 1048592 | tf_op jit(solution)/shard_map/reduce_scatter | solution.py:125
  951.9 2.1 fusion.17
  954.1 21.5 %all-reduce = (bf16[256]{0:T(256)(128)(2,1)S(1)}, bf16[3,256]{1,0:T(4,128)(2,1)S(1)}, bf16[256]{0:T(256)(128)(2,1)S(1)}) all-reduce(bf16[256]{0:T(256)(128)(2,1)S(1)} %get-tuple-element.14, bf16[3,256]{1,0:T(4,128)(2,1)S(1)} %pad_maximum_fusion.10, ...), channel_id=1, replica_groups=mesh['dp'=2,'seq'=4,'chan'=4] {'dp','seq'}, use_global_device_ids=true, to_apply=%region_10.0 | all-reduce | flops 1280 | bytes 5120 | tf_op jit(solution)/shard_map/psum | solution.py:139
  977.3 6.1 psum.79
  983.4 3.1 fusion.16
  (86 shorter events, 10.3 us)
Async XLA Ops:
  7.2 252.0 %copy-start = (bf16[1152,1024]{1,0:T(8,128)(2,1)S(1)}, bf16[1152,1024]{1,0:T(8,128)(2,1)}, u32[]{:S(2)}) copy-start(bf16[1152,1024]{1,0:T(8,128)(2,1)} %param.16) | copy-start | bytes 7077892
  7.2 3.4 copy-start.20
  7.2 40.1 %all-gather.4.cloned.1.call-start = ((), (), s32[]{:S(2)}) async-start(), calls=%async_computation.2 | async-start | bytes 5242880 | tf_op jit(solution)/shard_map/all_gather | solution.py:45
  7.9 214.5 %all-reduce.8.cloned.1.call-start = ((), (), s32[]{:S(2)}) async-start(), calls=%async_computation.3 | async-start | bytes 16777216 | tf_op jit(solution)/shard_map/psum | solution.py:65
  47.3 3.4 copy-start.7
  55.8 7.2 copy-start.4
  55.8 3.9 copy-start.18
  56.1 6.9 copy-start.5
  56.1 7.9 copy-start.14
  56.1 4.8 collective-permute-start
  63.0 1.0 copy-start.9
  68.6 1.3 copy-start.19
  68.6 190.6 %all-gather.6.cloned.1.call-start = ((), (), s32[]{:S(2)}) async-start(), calls=%async_computation.5 | async-start | bytes 5242880 | tf_op jit(solution)/shard_map/all_gather | solution.py:82
  69.4 376.9 %all-reduce.10.cloned.1.call-start = ((), (), s32[]{:S(2)}) async-start(), calls=%async_computation.6 | async-start | bytes 16777216 | tf_op jit(solution)/shard_map/psum | solution.py:92
  228.2 3.4 copy-start.2
  293.3 241.4 %all-reduce.12.cloned.1.call-start = ((), (), s32[]{:S(2)}) async-start(), calls=%async_computation.8 | async-start | bytes 3145728 | tf_op jit(solution)/shard_map/psum | solution.py:13
  446.3 8.2 copy-start.3
  446.3 18.4 %slice-start = ((s8[6291456]{0:T(1024)(128)(4,1)}), s8[4194304]{0:T(1024)(128)(4,1)S(1)}, s32[]{:S(2)}) async-start(s8[6291456]{0:T(1024)(128)(4,1)} %bitcast.24), calls=%async_computation.11 | async-start | bytes 8388608
  454.5 10.1 %slice-start.1 = ((s8[6291456]{0:T(1024)(128)(4,1)}), s8[2097152]{0:T(1024)(128)(4,1)S(1)}, s32[]{:S(2)}) async-start(s8[6291456]{0:T(1024)(128)(4,1)} %bitcast.24), calls=%async_computation.12 | async-start | bytes 4194304
  460.4 4.3 copy-start.1
  460.4 4.3 copy-start.6
  460.4 5.4 copy-start.12
  466.9 5.5 collective-permute-start.1
  473.2 8.0 copy-start.15
  473.2 2.9 copy-start.8
  473.5 7.6 copy-start.16
  483.8 122.2 %all-reduce.14.cloned.1.call-start = ((), (), s32[]{:S(2)}) async-start(), calls=%async_computation.9 | async-start | bytes 3145728 | tf_op jit(solution)/shard_map/psum | solution.py:13
  534.7 117.3 %reduce-scatter.3.cloned.1.call-start = ((), (), s32[]{:S(2)}) async-start(), calls=%async_computation.4 | async-start | bytes 5242880 | tf_op jit(solution)/shard_map/reduce_scatter | solution.py:75
  544.4 361.5 %all-reduce.16.cloned.1.call-start = ((), (), s32[]{:S(2)}) async-start(), calls=%async_computation.10 | async-start | bytes 15204352 | tf_op jit(solution)/shard_map/psum | solution.py:142
  571.6 9.4 copy-start.10
  586.5 365.4 %reduce-scatter.5.cloned.1.call-start = ((), (), s32[]{:S(2)}) async-start(), calls=%async_computation.7 | async-start | bytes 5242880 | tf_op jit(solution)/shard_map/reduce_scatter | solution.py:125
  594.3 0.7 copy-start.21
  905.8 7.3 copy-start.13
  913.1 3.0 copy-start.17
  913.1 38.8 %copy-start.11 = (bf16[2048,256]{1,0:T(8,128)(2,1)S(1)}, bf16[2048,256]{1,0:T(8,128)(2,1)}, u32[]{:S(2)}) copy-start(bf16[2048,256]{1,0:T(8,128)(2,1)} %param.9) | copy-start | bytes 3145732
Sparse Core Ops, SparseCore 0:
  9.6 37.7 all-gather.3
  68.8 153.6 all-reduce.7
  224.0 35.1 all-gather.5
  293.4 152.8 all-reduce.9
  483.9 50.7 all-reduce.11
  536.9 68.9 all-reduce.13
  608.5 43.5 reduce-scatter.2
  657.1 248.6 all-reduce.15
  908.3 43.5 reduce-scatter.4
